TPU v7x, 32 devices: a whole 2x2x4 slice. The times are simulated.
32 devices in a mesh: dp: 8 (over y, x, core), tensor: 4 (over z).
Axes of the slice: x: 2, y: 2, z: 4, core: 2. Of those that a mesh axis runs over, the one named last changes fastest.
Arguments:
- tokens: bfloat16 [8192, 2048], P(('dp', 'tensor')), may hold values from -6 to 6
- cotangent: bfloat16 [8192, 2048], P(('dp', 'tensor')), may hold values from -6 to 6
- norm_gains: float32 [2, 2048], replicated, may hold values from 0.1 to 1.9
- norm_shifts: float32 [2, 2048], replicated, may hold values from -4 to 4
- query_key_value_weight: bfloat16 [2048, 3, 2048], P(None, None, 'tensor'), may hold values from -0.125 to 0.125
- b_qv: float32 [2, 2048], P(None, 'tensor'), may hold values from -4 to 4
- output_weight: bfloat16 [2048, 2048], P('tensor'), may hold values from -0.375 to 0.375
- output_bias_vector: float32 [2048], replicated, may hold values from -4 to 4
- up_weight: bfloat16 [2048, 8192], P(None, 'tensor'), may hold values from -0.125 to 0.125
- b_up: float32 [8192], P('tensor'), may hold values from -4 to 4
- down_weight: bfloat16 [8192, 2048], P('tensor'), may hold values from -0.0625 to 0.0625
- down_bias_vector: float32 [2048], replicated, may hold values from -4 to 4
- adapter_query_key_value_input: bfloat16 [8, 16, 2048], replicated, may hold values from -0.125 to 0.125
- qkv_out: bfloat16 [8, 16, 3, 2048], P(None, None, None, 'tensor'), may hold values from -1.5 to 1.5
- adapter_output_input: bfloat16 [8, 16, 2048], P(None, None, 'tensor'), may hold values from -0.375 to 0.375
- adapter_output_output: bfloat16 [8, 16, 2048], replicated, may hold values from -1.5 to 1.5
- adapter_up_input: bfloat16 [8, 16, 2048], replicated, may hold values from -0.125 to 0.125
- up_out: bfloat16 [8, 16, 8192], P(None, None, 'tensor'), may hold values from -1.5 to 1.5
- down_in: bfloat16 [8, 16, 8192], P(None, None, 'tensor'), may hold values from -0.0625 to 0.0625
- adapter_down_output: bfloat16 [8, 16, 2048], replicated, may hold values from -1.5 to 1.5
- offsets: int32 [8, 2], P('dp'), may hold values from 0 to 768, as said below
- adapter_ids: int32 [8, 4], P('dp'), may hold values from 0 to 7
Outputs:
- out: bfloat16 [8192, 2048], P(('dp', 'tensor'))
- in_grad: bfloat16 [8192, 2048], P(('dp', 'tensor'))
- g_qkv_in: float32 [8, 16, 2048], replicated
- g_qkv_out: float32 [8, 16, 3, 2048], P(None, None, None, 'tensor')
- g_out_in: float32 [8, 16, 2048], P(None, None, 'tensor')
- g_out_out: float32 [8, 16, 2048], replicated
- g_up_in: float32 [8, 16, 2048], replicated
- g_up_out: float32 [8, 16, 8192], P(None, None, 'tensor')
- g_down_in: float32 [8, 16, 8192], P(None, None, 'tensor')
- g_down_out: float32 [8, 16, 2048], replicated
Inputs may be any that keep to these rules, and one draw needn't show every extreme that they name: For every sequence s, offsets[s, 0] + 256 <= offsets[s, 1]: the two pieces of 256 positions lie inside the sequence and don't intersect.
All inputs are finite; a program needn't handle non-finite values.
Results may differ from a plain program's by a relative error of at most 0.02.
Values may be sent and summed in bfloat16 or wider, within the bound.
A program may use at most 192 MiB of HBM per device.

v0:
```python
import math
import jax
import jax.numpy as jnp
from jax import lax
from jax.sharding import PartitionSpec as P

HEADS = 16
HEAD_DIM = 128
PIECE = 256
EPS = 1e-05
GELU_C = 0.7978845608028654
GELU_K = 0.044715
NEGATIVE = -1e30
EXACT_MODE = lax.Precision.HIGHEST


def layer_norm(values, gain_row, shift_row):
    centre = values - jnp.mean(values, axis=-1, keepdims=True)
    spread = jnp.mean(centre * centre, axis=-1, keepdims=True)
    inverse = lax.rsqrt(spread + EPS)
    scaled = centre * inverse
    return (scaled * gain_row + shift_row, scaled, inverse)


def norm_back(grad_rows, scaled, inverse, gain_row):
    inner_grad = grad_rows * gain_row
    first_mean = jnp.mean(inner_grad, axis=-1, keepdims=True)
    second_mean = jnp.mean(inner_grad * scaled, axis=-1, keepdims=True)
    return inverse * (inner_grad - first_mean - scaled * second_mean)


def gelu_parts(values):
    cubic = GELU_K * values * values * values
    tangent = jnp.tanh(GELU_C * (values + cubic))
    gelu_value = 0.5 * values * (1.0 + tangent)
    gelu_slope = 0.5 * (1.0 + tangent) + 0.5 * values * (1.0 - tangent * tangent) * GELU_C * (
        1.0 + 3.0 * GELU_K * values * values
    )
    return (gelu_value, gelu_slope)


def dot_transposed(left, right):
    return lax.dot_general(
        left, right, (((1,), (1,)), ((), ())), preferred_element_type=jnp.float32
    )


def choose(adapter_table, indicator_matrix):
    picked = jnp.einsum(
        "ge,erm->grm", indicator_matrix, adapter_table, preferred_element_type=jnp.float32
    )
    return picked.astype(jnp.bfloat16)


def low_rank_down(activations, chosen):
    shaped = activations.reshape(chosen.shape[0], -1, activations.shape[-1])
    return jnp.einsum("glm,grm->glr", shaped, chosen, preferred_element_type=jnp.float32)


def low_rank_upward(rank_rows, chosen):
    product = jnp.einsum(
        "glr,grm->glm", rank_rows, chosen.astype(jnp.float32), precision=EXACT_MODE
    )
    return product.reshape(-1, product.shape[-1])


def rank_grad(rank_rows, activations):
    shaped = activations.reshape(rank_rows.shape[0], -1, activations.shape[-1]).astype(jnp.float32)
    return jnp.einsum("glr,glm->grm", rank_rows, shaped, precision=EXACT_MODE)


def to_tables(per_sequence, indicator_matrix):
    return jnp.einsum("ge,grm->erm", indicator_matrix, per_sequence, precision=EXACT_MODE)


def block_scores(query_rows, key_rows, pieces, slopes, first_row):
    rows_here = query_rows.shape[1]
    length = key_rows.shape[1]
    keys_at = jnp.arange(length, dtype=jnp.int32)
    query_at = first_row + jnp.arange(rows_here, dtype=jnp.int32)
    scaling = 1.0 / math.sqrt(key_rows.shape[3])
    scores = (
        jnp.einsum("gqhd,gkhd->ghqk", query_rows, key_rows, preferred_element_type=jnp.float32)
        * scaling
    )
    distance = jnp.abs(query_at[:, None] - keys_at[None, :]).astype(jnp.float32)
    scores = scores - slopes[None, :, None, None] * distance[None, None]
    piece_rows = pieces[:, first_row : first_row + rows_here]
    allowed = (keys_at[None, None, :] <= query_at[None, :, None]) | (
        piece_rows[:, :, None] == pieces[:, None, :]
    ) & (piece_rows[:, :, None] > 0)
    return jnp.where(allowed[:, None], scores, NEGATIVE)


def attend(queries, key_rows, values, pieces, slopes):
    length = queries.shape[1]
    block_rows = min(512, length)
    contexts = []
    log_sums = []
    for first_row in range(0, length, block_rows):
        scores = block_scores(
            queries[:, first_row : first_row + block_rows], key_rows, pieces, slopes, first_row
        )
        row_peak = jnp.max(scores, axis=-1, keepdims=True)
        exponent = jnp.exp(scores - row_peak)
        total_sum = jnp.sum(exponent, axis=-1, keepdims=True)
        weights = (exponent / total_sum).astype(jnp.bfloat16)
        contexts.append(
            jnp.einsum("ghqk,gkhd->gqhd", weights, values, preferred_element_type=jnp.float32)
        )
        log_sums.append(row_peak + jnp.log(total_sum))
    return (jnp.concatenate(contexts, 1), jnp.concatenate(log_sums, 2))


def attend_back(queries, key_rows, values, pieces, slopes, log_sums, grad_context):
    length = queries.shape[1]
    block_rows = min(512, length)
    scaling = 1.0 / math.sqrt(key_rows.shape[3])
    grad_queries = []
    grad_keys = jnp.zeros(key_rows.shape, jnp.float32)
    grad_values = jnp.zeros(values.shape, jnp.float32)
    for first_row in range(0, length, block_rows):
        query_rows = queries[:, first_row : first_row + block_rows]
        grad_rows = grad_context[:, first_row : first_row + block_rows]
        scores = block_scores(query_rows, key_rows, pieces, slopes, first_row)
        probability = jnp.exp(scores - log_sums[:, :, first_row : first_row + block_rows])
        grad_values = grad_values + jnp.einsum(
            "ghqk,gqhd->gkhd",
            probability.astype(jnp.bfloat16),
            grad_rows,
            preferred_element_type=jnp.float32,
        )
        grad_probs = jnp.einsum(
            "gqhd,gkhd->ghqk", grad_rows, values, preferred_element_type=jnp.float32
        )
        inner_sum = jnp.sum(probability * grad_probs, axis=-1, keepdims=True)
        grad_scores = (probability * (grad_probs - inner_sum)).astype(jnp.bfloat16)
        grad_queries.append(
            jnp.einsum("ghqk,gkhd->gqhd", grad_scores, key_rows, preferred_element_type=jnp.float32)
            * scaling
        )
        grad_keys = (
            grad_keys
            + jnp.einsum(
                "ghqk,gqhd->gkhd", grad_scores, query_rows, preferred_element_type=jnp.float32
            )
            * scaling
        )
    return (jnp.concatenate(grad_queries, 1), grad_keys, grad_values)


def body(
    tokens,
    cotangent,
    norm_gains,
    norm_shifts,
    query_key_value_weight,
    b_qv,
    output_weight,
    output_bias_vector,
    up_weight,
    b_up,
    down_weight,
    down_bias_vector,
    adapter_query_key_value_input,
    qkv_out,
    adapter_output_input,
    adapter_output_output,
    adapter_up_input,
    up_out,
    down_in,
    adapter_down_output,
    offsets,
    adapter_ids,
):
    row_count = tokens.shape[0]
    model_width = tokens.shape[1]
    position = lax.axis_index("tensor")
    seq_count = offsets.shape[0]
    full_rows = row_count * lax.axis_size("tensor")
    length = full_rows // seq_count
    local_width = query_key_value_weight.shape[2]
    local_heads = local_width // HEAD_DIM
    table_count = adapter_query_key_value_input.shape[0]
    indicator_matrix = (
        adapter_ids[:, :, None] == jnp.arange(table_count, dtype=jnp.int32)[None, None, :]
    ).astype(jnp.float32)
    one_low = indicator_matrix.astype(jnp.bfloat16)
    chosen_qkv_in = choose(adapter_query_key_value_input, one_low[:, 0])
    chosen_qkv_out = choose(
        qkv_out.reshape(table_count, qkv_out.shape[1], 3 * local_width), one_low[:, 0]
    )
    chosen_out_in = choose(adapter_output_input, one_low[:, 1])
    chosen_out_out = choose(adapter_output_output, one_low[:, 1])
    chosen_up_in = choose(adapter_up_input, one_low[:, 2])
    chosen_up_out = choose(up_out, one_low[:, 2])
    chosen_down_in = choose(down_in, one_low[:, 3])
    chosen_down_out = choose(adapter_down_output, one_low[:, 3])
    where_at = jnp.arange(length, dtype=jnp.int32)
    first_piece = (
        (where_at[None, :] >= offsets[:, 0:1]) & (where_at[None, :] < offsets[:, 0:1] + PIECE)
    ).astype(jnp.int32)
    second_piece = (
        (where_at[None, :] >= offsets[:, 1:2]) & (where_at[None, :] < offsets[:, 1:2] + PIECE)
    ).astype(jnp.int32)
    pieces = first_piece + 2 * second_piece
    head_ids = (position * local_heads + jnp.arange(local_heads, dtype=jnp.int32)).astype(
        jnp.float32
    )
    slopes = jnp.exp2(-8.0 * (head_ids + 1.0) / HEADS)
    qkv_flat = query_key_value_weight.reshape(model_width, 3 * local_width)
    qkv_bias = jnp.concatenate([b_qv[0], jnp.zeros_like(b_qv[0]), b_qv[1]])
    inputs = tokens.astype(jnp.float32)
    normed_local, scaled_first, inverse_first = layer_norm(inputs, norm_gains[0], norm_shifts[0])
    sent_in = normed_local.astype(jnp.bfloat16)
    arrived = lax.all_gather(sent_in, "tensor", axis=0, tiled=True)
    low_rank_query_key_value = low_rank_down(arrived, chosen_qkv_in)
    projection_result = (
        jnp.dot(arrived, qkv_flat, preferred_element_type=jnp.float32)
        + low_rank_upward(low_rank_query_key_value, chosen_qkv_out)
        + qkv_bias
    )
    projection_result = projection_result.astype(jnp.bfloat16).reshape(
        seq_count, length, 3, local_heads, HEAD_DIM
    )
    queries = projection_result[:, :, 0]
    key_rows = projection_result[:, :, 1]
    values = projection_result[:, :, 2]
    attended_context, log_sums = attend(queries, key_rows, values, pieces, slopes)
    attended_context = attended_context.astype(jnp.bfloat16).reshape(full_rows, local_width)
    rank_ctx = low_rank_down(attended_context, chosen_out_in)
    ctx_term = low_rank_upward(rank_ctx, chosen_out_out)
    row_block = attended_context
    side_path = lax.psum_scatter(
        (jnp.dot(row_block, output_weight, preferred_element_type=jnp.float32) + ctx_term).astype(
            jnp.bfloat16
        ),
        "tensor",
        scatter_dimension=0,
        tiled=True,
    ).astype(jnp.float32)
    middle = inputs + (side_path + output_bias_vector)
    normed_mid_local, scaled_second, inverse_second = layer_norm(
        middle, norm_gains[1], norm_shifts[1]
    )
    normalized_middle = lax.all_gather(
        normed_mid_local.astype(jnp.bfloat16), "tensor", axis=0, tiled=True
    )
    rank_upper = low_rank_down(normalized_middle, chosen_up_in)
    gate_input_rows = (
        jnp.dot(normalized_middle, up_weight, preferred_element_type=jnp.float32)
        + low_rank_upward(rank_upper, chosen_up_out)
        + b_up
    )
    hidden_value, hidden_slope = gelu_parts(gate_input_rows)
    hidden_rows = hidden_value.astype(jnp.bfloat16)
    rank_lower = low_rank_down(hidden_rows, chosen_down_in)
    lower_term = low_rank_upward(rank_lower, chosen_down_out)
    row_block = hidden_rows
    mlp_part = lax.psum_scatter(
        (jnp.dot(row_block, down_weight, preferred_element_type=jnp.float32) + lower_term).astype(
            jnp.bfloat16
        ),
        "tensor",
        scatter_dimension=0,
        tiled=True,
    ).astype(jnp.float32)
    result = (middle + (mlp_part + down_bias_vector)).astype(jnp.bfloat16)
    grad_out = lax.all_gather(cotangent, "tensor", axis=0, tiled=True)
    grad_rank_lower = low_rank_down(grad_out, chosen_down_out)
    table_down_out = rank_grad(rank_lower, grad_out)
    table_down_in = rank_grad(grad_rank_lower, hidden_rows)
    grad_hidden = dot_transposed(grad_out, down_weight) + low_rank_upward(
        grad_rank_lower, chosen_down_in
    )
    grad_gate = (grad_hidden * hidden_slope).astype(jnp.bfloat16)
    grad_rank_upper = low_rank_down(grad_gate, chosen_up_out)
    table_up_out = rank_grad(rank_upper, grad_gate)
    table_up_in = rank_grad(grad_rank_upper, normalized_middle)
    upper_back = low_rank_upward(grad_rank_upper, chosen_up_in)
    row_block = grad_gate
    grad_mid_norm = lax.psum_scatter(
        (dot_transposed(row_block, up_weight) + upper_back).astype(jnp.bfloat16),
        "tensor",
        scatter_dimension=0,
        tiled=True,
    ).astype(jnp.float32)
    grad_middle = cotangent.astype(jnp.float32) + norm_back(
        grad_mid_norm, scaled_second, inverse_second, norm_gains[1]
    )
    grad_mid_low = lax.all_gather(grad_middle.astype(jnp.bfloat16), "tensor", axis=0, tiled=True)
    grad_rank_ctx = low_rank_down(grad_mid_low, chosen_out_out)
    table_out_out = rank_grad(rank_ctx, grad_mid_low)
    table_out_in = rank_grad(grad_rank_ctx, attended_context)
    grad_context = dot_transposed(grad_mid_low, output_weight) + low_rank_upward(
        grad_rank_ctx, chosen_out_in
    )
    grad_context = grad_context.astype(jnp.bfloat16).reshape(
        seq_count, length, local_heads, HEAD_DIM
    )
    grad_queries, grad_keys, grad_values = attend_back(
        queries, key_rows, values, pieces, slopes, log_sums, grad_context
    )
    grad_proj = (
        jnp.stack([grad_queries, grad_keys, grad_values], 2)
        .astype(jnp.bfloat16)
        .reshape(full_rows, 3 * local_width)
    )
    grad_rank_qkv = low_rank_down(grad_proj, chosen_qkv_out)
    table_qkv_out = rank_grad(low_rank_query_key_value, grad_proj)
    table_qkv_in = rank_grad(grad_rank_qkv, arrived)
    first_back = low_rank_upward(grad_rank_qkv, chosen_qkv_in)
    row_block = grad_proj
    grad_first = lax.psum_scatter(
        (dot_transposed(row_block, qkv_flat) + first_back).astype(jnp.bfloat16),
        "tensor",
        scatter_dimension=0,
        tiled=True,
    ).astype(jnp.float32)
    grad_tokens = (
        grad_middle + norm_back(grad_first, scaled_first, inverse_first, norm_gains[0])
    ).astype(jnp.bfloat16)
    shared = lax.psum(
        (
            to_tables(table_qkv_in, indicator_matrix[:, 0]),
            to_tables(table_out_out, indicator_matrix[:, 1]),
            to_tables(table_up_in, indicator_matrix[:, 2]),
            to_tables(table_down_out, indicator_matrix[:, 3]),
        ),
        ("dp", "tensor"),
    )
    owned_sums = (
        lax.psum(
            to_tables(table_qkv_out, indicator_matrix[:, 0])
            .reshape(qkv_out.shape)
            .astype(jnp.bfloat16),
            "dp",
        ).astype(jnp.float32),
        lax.psum(to_tables(table_out_in, indicator_matrix[:, 1]).astype(jnp.bfloat16), "dp").astype(
            jnp.float32
        ),
        lax.psum(to_tables(table_up_out, indicator_matrix[:, 2]).astype(jnp.bfloat16), "dp").astype(
            jnp.float32
        ),
        lax.psum(
            to_tables(table_down_in, indicator_matrix[:, 3]).astype(jnp.bfloat16), "dp"
        ).astype(jnp.float32),
    )
    return (
        result,
        grad_tokens,
        shared[0],
        owned_sums[0],
        owned_sums[1],
        shared[1],
        shared[2],
        owned_sums[2],
        owned_sums[3],
        shared[3],
    )


def solution(mesh):
    placed = (
        P(("dp", "tensor"), None),
        P(("dp", "tensor"), None),
        P(),
        P(),
        P(None, None, "tensor"),
        P(None, "tensor"),
        P("tensor", None),
        P(),
        P(None, "tensor"),
        P("tensor"),
        P("tensor", None),
        P(),
        P(),
        P(None, None, None, "tensor"),
        P(None, None, "tensor"),
        P(),
        P(),
        P(None, None, "tensor"),
        P(None, None, "tensor"),
        P(),
        P("dp", None),
        P("dp", None),
    )
    return jax.shard_map(
        body,
        mesh=mesh,
        in_specs=placed,
        out_specs=(
            P(("dp", "tensor"), None),
            P(("dp", "tensor"), None),
            P(),
            P(None, None, None, "tensor"),
            P(None, None, "tensor"),
            P(),
            P(),
            P(None, None, "tensor"),
            P(None, None, "tensor"),
            P(),
        ),
        check_vma=False,
    )
```

profile of v0, /device:TPU:0, one launch (start us, length us, event | category | flops | bytes accessed | tf_op | source)
XLA Modules:
  0.0 1041.3 jit_solution(12768031125403590012)
XLA Ops:
  17.7 9.0 copy.45
  38.1 60.4 %all-gather.5.cloned.1.call-done = bf16[1024,2048]{1,0:T(8,128)(2,1)} async-done(((bf16[256,2048]{1,0:T(8,128)(2,1)}), bf16[1024,2048]{1,0:T(8,128)(2,1)}) %all-gather.5.cloned.1.call-update) | async-done | bytes 4194320 | tf_op jit(solution)/shard_map/all_gather | solution.py:216
  102.0 8.8 fusion.112
  110.9 4.5 add_convert_fusion.4
  115.4 6.2 reshape.957
  121.6 4.2 fusion.104
  130.3 4.5 fusion.110
  151.7 5.6 add_convert_fusion.3
  158.2 74.7 %reduce-scatter.5.cloned.1.call-done = bf16[256,2048]{1,0:T(8,128)(2,1)} async-done(((bf16[1024,2048]{1,0:T(8,128)(2,1)}), bf16[256,2048]{1,0:T(8,128)(2,1)}) %reduce-scatter.5.cloned.1.call-update) | async-done | bytes 1048592 | tf_op jit(solution)/shard_map/reduce_scatter | solution.py:234
  245.7 70.1 %all-gather.9.cloned.1.call-done = bf16[1024,2048]{1,0:T(8,128)(2,1)} async-done(((bf16[256,2048]{1,0:T(8,128)(2,1)}), bf16[1024,2048]{1,0:T(8,128)(2,1)}) %all-gather.9.cloned.1.call-update) | async-done | bytes 4194320 | tf_op jit(solution)/shard_map/all_gather | solution.py:269
  315.8 4.2 fusion.74
  320.0 13.4 %fusion.115 = f32[1024,2048]{1,0:T(8,128)} fusion(bf16[1024,2048]{1,0:T(8,128)(2,1)S(1)} %copy-done.14, bf16[2048,2048]{1,0:T(8,128)(2,1)} %param.32), kind=kOutput, calls=%fused_computation.205 | convolution fusion | flops 8589934592 | bytes 20971520 | tf_op jit(solution)/shard_map/dot_general | solution.py:43
  333.4 63.8 %all-gather.7.cloned.1.call-done = bf16[1024,2048]{1,0:T(8,128)(2,1)} async-done(((bf16[256,2048]{1,0:T(8,128)(2,1)}), bf16[1024,2048]{1,0:T(8,128)(2,1)}) %all-gather.7.cloned.1.call-update) | async-done | bytes 4194320 | tf_op jit(solution)/shard_map/all_gather | solution.py:246
  400.8 13.3 %fusion.113 = f32[1024,2048]{1,0:T(8,128)} fusion(bf16[1024,2048]{1,0:T(8,128)(2,1)S(1)} %copy-done.9, bf16[2048,2048]{1,0:T(8,128)(2,1)} %param.30), kind=kOutput, calls=%fused_computation.203 | convolution fusion | flops 8589934592 | bytes 20971520 | tf_op jit(solution)/shard_map/dot_general | solution.py:251
  414.1 10.2 multiply_convert_fusion.2
  424.3 11.1 %fusion.6 = bf16[1024,2048]{1,0:T(8,128)(2,1)S(1)} fusion(f32[1024,2048]{1,0:T(8,128)S(1)} %get-tuple-element.55, f32[1024,2048]{1,0:T(8,128)} %fusion.115, f32[16,1024]{1,0:T(8,128)S(1)} %copy-done.49, bf16[1,16,2048]{2,0,1:T(2,128)(2,1)S(1)} %copy-done.45), kind=kOutput, calls=%fused_computation.8 | convolution fusion | flops 444596224 | bytes 21102592 | tf_op jit(solution)/shard_map/glr,grm->glm/dot_general | solution.py:61
  436.7 8.8 fusion.116
  445.5 5.3 add_convert_fusion.1
  454.8 11.9 %fusion.114 = f32[1024,2048]{1,0:T(8,128)S(1)} fusion(bf16[1024,2048]{1,0:T(8,128)(2,1)S(1)} %copy-done.13, bf16[2048,2048]{1,0:T(8,128)(2,1)} %param.32), kind=kOutput, calls=%fused_computation.204 | convolution fusion | flops 8589934592 | bytes 20971520 | tf_op jit(solution)/shard_map/dot_general | solution.py:261
  466.7 5.5 add_convert_fusion.2
  472.3 54.0 %reduce-scatter.9.cloned.1.call-done = bf16[256,2048]{1,0:T(8,128)(2,1)} async-done(((bf16[1024,2048]{1,0:T(8,128)(2,1)}), bf16[256,2048]{1,0:T(8,128)(2,1)}) %reduce-scatter.9.cloned.1.call-update) | async-done | bytes 1048592 | tf_op jit(solution)/shard_map/reduce_scatter | solution.py:282
  528.7 77.0 %reduce-scatter.7.cloned.1.call-done = bf16[256,2048]{1,0:T(8,128)(2,1)} async-done(((bf16[1024,2048]{1,0:T(8,128)(2,1)}), bf16[256,2048]{1,0:T(8,128)(2,1)}) %reduce-scatter.7.cloned.1.call-update) | async-done | bytes 1048592 | tf_op jit(solution)/shard_map/reduce_scatter | solution.py:260
  605.7 5.7 fusion.103
  614.5 4.1 fusion.123
  626.6 66.4 %all-gather.11.cloned.1.call-done = bf16[1024,2048]{1,0:T(8,128)(2,1)} async-done(((bf16[256,2048]{1,0:T(8,128)(2,1)}), bf16[1024,2048]{1,0:T(8,128)(2,1)}) %all-gather.11.cloned.1.call-update) | async-done | bytes 4194320 | tf_op jit(solution)/shard_map/all_gather | solution.py:291
  716.5 3.9 add_bitcast_fusion
  728.4 9.5 fusion.118
  742.0 7.7 add_convert_fusion
  750.5 4.1 fusion.120
  758.7 38.8 %all-reduce.7.cloned.1.call-done = (bf16[8,16,3,512]{3,1,2,0:T(8,128)(2,1)}, bf16[8,16,512]{2,1,0:T(8,128)(2,1)}, bf16[8,16,2048]{2,1,0:T(8,128)(2,1)}, bf16[8,16,2048]{2,1,0:T(8,128)(2,1)}) async-done(((bf16[8,16,3,512]{3,1,2,0:T(8,128)(2,1)}, bf16[8,16,512]{2,1,0:T(8,128)(2,1)}, bf16[8,16,2048]{2,1,0:T(8,128)(2,1)}, bf16[8,16,2048]{2,1,0:T(8,128)(2,1)}), (bf16[8,16,3,512]{3,1,2,0:T(8,128)(2,1)}, ...) | async-done | bytes 1572880 | tf_op jit(solution)/shard_map/psum | solution.py:333
  805.4 70.6 %reduce-scatter.11.cloned.1.call-done = bf16[256,2048]{1,0:T(8,128)(2,1)} async-done(((bf16[1024,2048]{1,0:T(8,128)(2,1)}), bf16[256,2048]{1,0:T(8,128)(2,1)}) %reduce-scatter.11.cloned.1.call-update) | async-done | bytes 1048592 | tf_op jit(solution)/shard_map/reduce_scatter | solution.py:314
  881.7 145.7 %all-reduce.5.cloned.1.call-done = (f32[8,16,2048]{2,1,0:T(8,128)}, f32[8,16,2048]{2,1,0:T(8,128)}, f32[8,16,2048]{2,1,0:T(8,128)}, f32[8,16,2048]{2,1,0:T(8,128)}) async-done(((f32[8,16,2048]{2,1,0:T(8,128)}, f32[8,16,2048]{2,1,0:T(8,128)}, f32[8,16,2048]{2,1,0:T(8,128)}, f32[8,16,2048]{2,1,0:T(8,128)}), (f32[8,16,2048]{2,1,0:T(8,128)}, f32[8,16,2048]{2,1,0:T(8,128)}, f32[8,16,2048]{2,1,0:T(8,128)}, ...) | async-done | bytes 4194320 | tf_op jit(solution)/shard_map/psum | solution.py:323
  (296 shorter events, 141.1 us)
Async XLA Ops:
  7.2 142.1 %copy-start = (bf16[512,2048]{1,0:T(8,128)(2,1)S(1)}, bf16[512,2048]{1,0:T(8,128)(2,1)}, u32[]{:S(2)}) copy-start(bf16[512,2048]{1,0:T(8,128)(2,1)} %param.28) | copy-start | bytes 6291460
  7.2 91.3 %all-gather.5.cloned.1.call-start = ((), (), s32[]{:S(2)}) async-start(), calls=%async_computation.4 | async-start | bytes 5242880 | tf_op jit(solution)/shard_map/all_gather | solution.py:216
  8.9 17.9 %copy-start.64 = (f32[256]{0:T(256)}, f32[256]{0:T(256)S(1)}, u32[]{:S(2)}) copy-start(f32[256]{0:T(256)S(1)} %broadcast_multiply_fusion.9) | copy-start | bytes 3076
  10.5 16.2 %copy-start.66 = (f32[256]{0:T(256)}, f32[256]{0:T(256)S(1)}, u32[]{:S(2)}) copy-start(f32[256]{0:T(256)S(1)} %add_rsqrt_fusion.1) | copy-start | bytes 3076
  11.4 15.4 %copy-start.52 = (f32[1,2048]{1,0:T(1,128)}, f32[1,2048]{1,0:T(1,128)S(1)}, u32[]{:S(2)}) copy-start(f32[1,2048]{1,0:T(1,128)S(1)} %get-tuple-element.28) | copy-start | bytes 24580
  14.9 218.0 %reduce-scatter.5.cloned.1.call-start = ((), (), s32[]{:S(2)}) async-start(), calls=%async_computation.5 | async-start | bytes 5242880 | tf_op jit(solution)/shard_map/reduce_scatter | solution.py:234
  17.7 13.9 %copy-start.54 = (bf16[8,16,512]{2,1,0:T(8,128)(2,1)S(1)}, bf16[8,16,512]{2,1,0:T(8,128)(2,1)}, u32[]{:S(2)}) copy-start(bf16[8,16,512]{2,1,0:T(8,128)(2,1)} %param.36) | copy-start | bytes 393220
  17.7 14.4 %copy-start.38 = (bf16[8,16,2048]{2,1,0:T(8,128)(2,1)S(1)}, bf16[8,16,2048]{2,1,0:T(8,128)(2,1)}, u32[]{:S(2)}) copy-start(bf16[8,16,2048]{2,1,0:T(8,128)(2,1)} %param.37) | copy-start | bytes 1572868
  31.6 206.5 %copy-start.55 = (bf16[1,4,8]{2,1,0:T(4,128)(2,1)}, bf16[1,4,8]{2,1,0:T(4,128)(2,1)S(1)}, u32[]{:S(2)}) copy-start(bf16[1,4,8]{2,1,0:T(4,128)(2,1)S(1)} %get-tuple-element.47) | copy-start | bytes 196
  31.9 117.1 %copy-start.56 = (bf16[1,16,512]{2,0,1:T(2,128)(2,1)}, bf16[1,16,512]{2,0,1:T(2,128)(2,1)S(1)}, u32[]{:S(2)}) copy-start(bf16[1,16,512]{2,0,1:T(2,128)(2,1)S(1)} %fusion.65) | copy-start | bytes 49156
  32.1 78.7 %copy-start.40 = (bf16[1,16,1536]{2,0,1:T(2,128)(2,1)}, bf16[1,16,1536]{2,0,1:T(2,128)(2,1)S(1)}, u32[]{:S(2)}) copy-start(bf16[1,16,1536]{2,0,1:T(2,128)(2,1)S(1)} %fusion.89) | copy-start | bytes 147460
  34.1 67.9 %copy-start.34 = (bf16[1,16,2048]{2,0,1:T(2,128)(2,1)}, bf16[1,16,2048]{2,0,1:T(2,128)(2,1)S(1)}, u32[]{:S(2)}) copy-start(bf16[1,16,2048]{2,0,1:T(2,128)(2,1)S(1)} %fusion.59) | copy-start | bytes 196612
  125.8 14.7 %copy-start.16 = (bf16[1,1024,1,4,128]{4,3,2,1,0:T(4,128)(2,1)}, bf16[1,1024,1,4,128]{4,3,2,1,0:T(4,128)(2,1)S(1)}, u32[]{:S(2)}) copy-start(bf16[1,1024,1,4,128]{4,3,2,1,0:T(4,128)(2,1)S(1)} %get-tuple-element.25) | copy-start | bytes 3145732
  157.3 75.5 %copy-start.3 = (bf16[256,2048]{1,0:T(8,128)(2,1)S(1)}, bf16[256,2048]{1,0:T(8,128)(2,1)}, u32[]{:S(2)}) copy-start(bf16[256,2048]{1,0:T(8,128)(2,1)} %param.22) | copy-start | bytes 3145732
  157.3 75.5 %copy-start.51 = (f32[2048]{0:T(1024)S(1)}, f32[2048]{0:T(1024)}, u32[]{:S(2)}) copy-start(f32[2048]{0:T(1024)} %param.29) | copy-start | bytes 24580
  157.4 158.4 %all-gather.9.cloned.1.call-start = ((), (), s32[]{:S(2)}) async-start(), calls=%async_computation.8 | async-start | bytes 5242880 | tf_op jit(solution)/shard_map/all_gather | solution.py:269
  158.1 239.1 %all-gather.7.cloned.1.call-start = ((), (), s32[]{:S(2)}) async-start(), calls=%async_computation.6 | async-start | bytes 5242880 | tf_op jit(solution)/shard_map/all_gather | solution.py:246
  238.1 288.2 %reduce-scatter.9.cloned.1.call-start = ((), (), s32[]{:S(2)}) async-start(), calls=%async_computation.9 | async-start | bytes 5242880 | tf_op jit(solution)/shard_map/reduce_scatter | solution.py:282
  245.7 151.5 %copy-start.36 = (bf16[1,16,2048]{2,0,1:T(2,128)(2,1)}, bf16[1,16,2048]{2,0,1:T(2,128)(2,1)S(1)}, u32[]{:S(2)}) copy-start(bf16[1,16,2048]{2,0,1:T(2,128)(2,1)S(1)} %fusion.55) | copy-start | bytes 196612
  414.1 22.5 %slice-start.6 = ((s8[8388608]{0:T(1024)(128)(4,1)}), s8[4194304]{0:T(1024)(128)(4,1)S(1)}, s32[]{:S(2)}) async-start(s8[8388608]{0:T(1024)(128)(4,1)} %bitcast.268), calls=%async_computation.20 | async-start | bytes 8388608
  450.9 154.9 %reduce-scatter.7.cloned.1.call-start = ((), (), s32[]{:S(2)}) async-start(), calls=%async_computation.7 | async-start | bytes 5242880 | tf_op jit(solution)/shard_map/reduce_scatter | solution.py:260
  472.2 54.1 %copy-start.63 = (f32[256]{0:T(256)S(1)}, f32[256]{0:T(256)}, u32[]{:S(2)}) copy-start(f32[256]{0:T(256)} %copy-done.62) | copy-start | bytes 3076
  472.2 54.1 %copy-start.69 = (f32[256]{0:T(256)S(1)}, f32[256]{0:T(256)}, u32[]{:S(2)}) copy-start(f32[256]{0:T(256)} %copy-done.68) | copy-start | bytes 3076
  472.2 133.5 %copy-start.70 = (f32[2048]{0:T(1024)S(1)}, f32[2048]{0:T(1024)}, u32[]{:S(2)}) copy-start(f32[2048]{0:T(1024)} %param.33) | copy-start | bytes 24580
  472.2 220.7 %all-gather.11.cloned.1.call-start = ((), (), s32[]{:S(2)}) async-start(), calls=%async_computation.10 | async-start | bytes 5242880 | tf_op jit(solution)/shard_map/all_gather | solution.py:291
  528.7 85.8 %copy-start.50 = (f32[16,1024]{1,0:T(8,128)S(1)}, f32[16,1024]{1,0:T(8,128)}, u32[]{:S(2)}) copy-start(f32[16,1024]{1,0:T(8,128)} %fusion.74) | copy-start | bytes 196612
  611.5 186.1 %all-reduce.7.cloned.1.call-start = ((), (), s32[]{:S(2)}) async-start(), calls=%async_computation.13 | async-start | bytes 3145728 | tf_op jit(solution)/shard_map/psum | solution.py:333
  739.5 136.5 %reduce-scatter.11.cloned.1.call-start = ((), (), s32[]{:S(2)}) async-start(), calls=%async_computation.11 | async-start | bytes 5242880 | tf_op jit(solution)/shard_map/reduce_scatter | solution.py:314
  749.7 277.6 %all-reduce.5.cloned.1.call-start = ((), (), s32[]{:S(2)}) async-start(), calls=%async_computation.12 | async-start | bytes 8388608 | tf_op jit(solution)/shard_map/psum | solution.py:323
  758.7 117.4 %copy-start.53 = (f32[1,2048]{1,0:T(1,128)S(1)}, f32[1,2048]{1,0:T(1,128)}, u32[]{:S(2)}) copy-start(f32[1,2048]{1,0:T(1,128)} %copy-done.52) | copy-start | bytes 24580
  758.7 117.4 %copy-start.65 = (f32[256]{0:T(256)S(1)}, f32[256]{0:T(256)}, u32[]{:S(2)}) copy-start(f32[256]{0:T(256)} %copy-done.64) | copy-start | bytes 3076
  758.7 117.4 %copy-start.67 = (f32[256]{0:T(256)S(1)}, f32[256]{0:T(256)}, u32[]{:S(2)}) copy-start(f32[256]{0:T(256)} %copy-done.66) | copy-start | bytes 3076
  (67 other events, 367.0 us)
Sparse Core Ops, SparseCore 0:
  15.0 83.4 all-gather.4
  157.5 75.2 reduce-scatter.4
  234.5 81.2 all-gather.8
  317.9 79.2 all-gather.6
  451.0 75.2 reduce-scatter.8
  528.5 77.2 reduce-scatter.6
  611.6 81.2 all-gather.10
  739.7 57.8 all-reduce.6
  799.9 76.1 reduce-scatter.10
  883.9 143.3 all-reduce.4
where the time goes:
time: 1050 us; the launch traced here: 1040 us
  waiting for transfers between devices  722 us (69%)
  matrix products  203 us (19%)
  other arithmetic  58.5 us (6%)
  local copies, waits for them, and re-layouts  39.8 us (4%)
  between operations  17 us (2%)
    psum x1, waiting for transfers between devices, body(): lax.psum((to_tables(table_qkv_in, indicator_matrix[:, 0]), to_tables(tabl...  146 us
    reduce_scatter x1, waiting for transfers between devices, body(): lax.psum_scatter((jnp.dot(row_block, down_weight, preferred_element_type=...  77 us
    reduce_scatter x1, waiting for transfers between devices, body(): lax.psum_scatter((jnp.dot(row_block, output_weight, preferred_element_typ...  74.7 us
    reduce_scatter x1, waiting for transfers between devices, body(): lax.psum_scatter((dot_transposed(row_block, qkv_flat) + first_back).astyp...  70.6 us
    all_gather x1, waiting for transfers between devices, body(): grad_out = lax.all_gather(cotangent, 'tensor', axis=0, tiled=True)  70.1 us
    all_gather x1, waiting for transfers between devices, body(): lax.all_gather(grad_middle.astype(jnp.bfloat16), 'tensor', axis=0, tiled=...  66.4 us
    all_gather x1, waiting for transfers between devices, body(): lax.all_gather(normed_mid_local.astype(jnp.bfloat16), 'tensor', axis=0, t...  63.8 us
    all_gather x1, waiting for transfers between devices, body(): arrived = lax.all_gather(sent_in, 'tensor', axis=0, tiled=True)  60.4 us
  transfers between devices with their start and end apart: 10, of which 10 were waited for; matrix products, arithmetic and copies ran while one was open for 12% of the time, Pallas kernels for 0%

commit v1 on v0

--- a/solution.py
+++ b/solution.py
@@ -321,13 +321,16 @@
         grad_middle + norm_back(grad_first, scaled_first, inverse_first, norm_gains[0])
     ).astype(jnp.bfloat16)
     shared = lax.psum(
-        (
-            to_tables(table_qkv_in, indicator_matrix[:, 0]),
-            to_tables(table_out_out, indicator_matrix[:, 1]),
-            to_tables(table_up_in, indicator_matrix[:, 2]),
-            to_tables(table_down_out, indicator_matrix[:, 3]),
-        ),
-        ("dp", "tensor"),
+        lax.psum(
+            (
+                to_tables(table_qkv_in, indicator_matrix[:, 0]),
+                to_tables(table_out_out, indicator_matrix[:, 1]),
+                to_tables(table_up_in, indicator_matrix[:, 2]),
+                to_tables(table_down_out, indicator_matrix[:, 3]),
+            ),
+            "tensor",
+        ),
+        "dp",
     )
     owned_sums = (
         lax.psum(

time: 1050 us -> 1140 us (1.086)
  waiting for transfers between devices: 722 us -> 810 us
    psum x0 -> x1, waiting for transfers between devices: none -> 80 us  [body(): lax.psum(lax.psum((to_tables(table_qkv_in, indicator_matrix[:, 0]), to_ta...]
    psum x1, waiting for transfers between devices: 38.8 us -> 62.5 us  [body(): lax.psum(to_tables(table_qkv_out, indicator_matrix[:, 0]).reshape(qkv_out...]
    psum x1, waiting for transfers between devices: 146 us -> 130 us  [body(): lax.psum((to_tables(table_qkv_in, indicator_matrix[:, 0]), to_tables(tabl...]
    unnamed x185 -> x177, local copies, waits for them, and re-layouts: 26.3 us -> 27.5 us
  transfers between devices with their start and end apart: 10 -> 11, of which waited for: 10 -> 11; matrix products, arithmetic and copies ran while one was open for 12% -> 11% of each run, Pallas kernels for 0% -> 0%
where the time goes in v1:
time: 1140 us; the launch traced here: 1130 us
  waiting for transfers between devices  810 us (71%)
  matrix products  203 us (18%)
  other arithmetic  58.8 us (5%)
  local copies, waits for them, and re-layouts  41.1 us (4%)
  between operations  16.8 us (1%)
    psum x1, waiting for transfers between devices, body(): lax.psum((to_tables(table_qkv_in, indicator_matrix[:, 0]), to_tables(tabl...  130 us
    psum x1, waiting for transfers between devices, body(): lax.psum(lax.psum((to_tables(table_qkv_in, indicator_matrix[:, 0]), to_ta...  80 us
    reduce_scatter x1, waiting for transfers between devices, body(): lax.psum_scatter((jnp.dot(row_block, down_weight, preferred_element_type=...  77 us
    reduce_scatter x1, waiting for transfers between devices, body(): lax.psum_scatter((jnp.dot(row_block, output_weight, preferred_element_typ...  74.7 us
    reduce_scatter x1, waiting for transfers between devices, body(): lax.psum_scatter((dot_transposed(row_block, qkv_flat) + first_back).astyp...  70.6 us
    all_gather x1, waiting for transfers between devices, body(): grad_out = lax.all_gather(cotangent, 'tensor', axis=0, tiled=True)  70.1 us
    all_gather x1, waiting for transfers between devices, body(): lax.all_gather(grad_middle.astype(jnp.bfloat16), 'tensor', axis=0, tiled=...  66.3 us
    all_gather x1, waiting for transfers between devices, body(): lax.all_gather(normed_mid_local.astype(jnp.bfloat16), 'tensor', axis=0, t...  63.8 us
  transfers between devices with their start and end apart: 11, of which 11 were waited for; matrix products, arithmetic and copies ran while one was open for 11% of the time, Pallas kernels for 0%

profile of v1, /device:TPU:0, one launch (start us, length us, event | category | flops | bytes accessed | tf_op | source)
XLA Modules:
  0.0 1130.8 jit_solution(16753168843215557092)
XLA Ops:
  17.7 9.0 copy.45
  38.1 60.4 %all-gather.5.cloned.1.call-done = bf16[1024,2048]{1,0:T(8,128)(2,1)} async-done(((bf16[256,2048]{1,0:T(8,128)(2,1)}), bf16[1024,2048]{1,0:T(8,128)(2,1)}) %all-gather.5.cloned.1.call-update) | async-done | bytes 4194320 | tf_op jit(solution)/shard_map/all_gather | solution.py:216
  102.0 8.8 fusion.112
  110.9 4.5 add_convert_fusion.4
  115.4 6.2 reshape.957
  121.6 4.2 fusion.104
  130.3 4.5 fusion.110
  151.7 5.6 add_convert_fusion.3
  158.1 74.7 %reduce-scatter.5.cloned.1.call-done = bf16[256,2048]{1,0:T(8,128)(2,1)} async-done(((bf16[1024,2048]{1,0:T(8,128)(2,1)}), bf16[256,2048]{1,0:T(8,128)(2,1)}) %reduce-scatter.5.cloned.1.call-update) | async-done | bytes 1048592 | tf_op jit(solution)/shard_map/reduce_scatter | solution.py:234
  245.6 70.1 %all-gather.9.cloned.1.call-done = bf16[1024,2048]{1,0:T(8,128)(2,1)} async-done(((bf16[256,2048]{1,0:T(8,128)(2,1)}), bf16[1024,2048]{1,0:T(8,128)(2,1)}) %all-gather.9.cloned.1.call-update) | async-done | bytes 4194320 | tf_op jit(solution)/shard_map/all_gather | solution.py:269
  315.8 4.2 fusion.74
  319.9 13.4 %fusion.115 = f32[1024,2048]{1,0:T(8,128)} fusion(bf16[1024,2048]{1,0:T(8,128)(2,1)S(1)} %copy-done.14, bf16[2048,2048]{1,0:T(8,128)(2,1)} %param.32), kind=kOutput, calls=%fused_computation.205 | convolution fusion | flops 8589934592 | bytes 20971520 | tf_op jit(solution)/shard_map/dot_general | solution.py:43
  333.3 63.8 %all-gather.7.cloned.1.call-done = bf16[1024,2048]{1,0:T(8,128)(2,1)} async-done(((bf16[256,2048]{1,0:T(8,128)(2,1)}), bf16[1024,2048]{1,0:T(8,128)(2,1)}) %all-gather.7.cloned.1.call-update) | async-done | bytes 4194320 | tf_op jit(solution)/shard_map/all_gather | solution.py:246
  400.7 13.3 %fusion.113 = f32[1024,2048]{1,0:T(8,128)} fusion(bf16[1024,2048]{1,0:T(8,128)(2,1)S(1)} %copy-done.8, bf16[2048,2048]{1,0:T(8,128)(2,1)} %param.30), kind=kOutput, calls=%fused_computation.203 | convolution fusion | flops 8589934592 | bytes 20971520 | tf_op jit(solution)/shard_map/dot_general | solution.py:251
  414.1 10.2 multiply_convert_fusion.2
  424.3 11.1 fusion.6
  436.6 8.8 fusion.116
  445.5 5.3 add_convert_fusion.1
  454.8 11.9 %fusion.114 = f32[1024,2048]{1,0:T(8,128)S(1)} fusion(bf16[1024,2048]{1,0:T(8,128)(2,1)S(1)} %copy-done.13, bf16[2048,2048]{1,0:T(8,128)(2,1)} %param.32), kind=kOutput, calls=%fused_computation.204 | convolution fusion | flops 8589934592 | bytes 20971520 | tf_op jit(solution)/shard_map/dot_general | solution.py:261
  466.6 5.5 add_convert_fusion.2
  472.2 54.0 %reduce-scatter.9.cloned.1.call-done = bf16[256,2048]{1,0:T(8,128)(2,1)} async-done(((bf16[1024,2048]{1,0:T(8,128)(2,1)}), bf16[256,2048]{1,0:T(8,128)(2,1)}) %reduce-scatter.9.cloned.1.call-update) | async-done | bytes 1048592 | tf_op jit(solution)/shard_map/reduce_scatter | solution.py:282
  528.7 77.0 %reduce-scatter.7.cloned.1.call-done = bf16[256,2048]{1,0:T(8,128)(2,1)} async-done(((bf16[1024,2048]{1,0:T(8,128)(2,1)}), bf16[256,2048]{1,0:T(8,128)(2,1)}) %reduce-scatter.7.cloned.1.call-update) | async-done | bytes 1048592 | tf_op jit(solution)/shard_map/reduce_scatter | solution.py:260
  605.7 5.7 fusion.103
  626.5 66.3 %all-gather.11.cloned.1.call-done = bf16[1024,2048]{1,0:T(8,128)(2,1)} async-done(((bf16[256,2048]{1,0:T(8,128)(2,1)}), bf16[1024,2048]{1,0:T(8,128)(2,1)}) %all-gather.11.cloned.1.call-update) | async-done | bytes 4194320 | tf_op jit(solution)/shard_map/all_gather | solution.py:291
  696.4 4.7 fusion.117
  738.7 5.1 fusion.67
  744.8 10.3 fusion.118
  755.2 5.6 add_convert_fusion
  760.8 129.7 %all-reduce.9.cloned.1.call-done = (f32[8,16,2048]{2,1,0:T(8,128)}, f32[8,16,2048]{2,1,0:T(8,128)}, f32[8,16,2048]{2,1,0:T(8,128)}, f32[8,16,2048]{2,1,0:T(8,128)}) async-done(((f32[8,16,2048]{2,1,0:T(8,128)}, f32[8,16,2048]{2,1,0:T(8,128)}, f32[8,16,2048]{2,1,0:T(8,128)}, f32[8,16,2048]{2,1,0:T(8,128)}), (f32[8,16,2048]{2,1,0:T(8,128)}, f32[8,16,2048]{2,1,0:T(8,128)}, f32[8,16,2048]{2,1,0:T(8,128)}, ...) | async-done | bytes 4194320 | tf_op jit(solution)/shard_map/psum | solution.py:324
  890.5 62.5 %all-reduce.11.cloned.1.call-done = (bf16[8,16,3,512]{3,1,2,0:T(8,128)(2,1)}, bf16[8,16,512]{2,1,0:T(8,128)(2,1)}, bf16[8,16,2048]{2,1,0:T(8,128)(2,1)}, bf16[8,16,2048]{2,1,0:T(8,128)(2,1)}) async-done(((bf16[8,16,3,512]{3,1,2,0:T(8,128)(2,1)}, bf16[8,16,512]{2,1,0:T(8,128)(2,1)}, bf16[8,16,2048]{2,1,0:T(8,128)(2,1)}, bf16[8,16,2048]{2,1,0:T(8,128)(2,1)}), (bf16[8,16,3,512]{3,1,2,0:T(8,128)(2,1)}, ...) | async-done | bytes 1572880 | tf_op jit(solution)/shard_map/psum | solution.py:336
  960.8 70.6 %reduce-scatter.11.cloned.1.call-done = bf16[256,2048]{1,0:T(8,128)(2,1)} async-done(((bf16[1024,2048]{1,0:T(8,128)(2,1)}), bf16[256,2048]{1,0:T(8,128)(2,1)}) %reduce-scatter.11.cloned.1.call-update) | async-done | bytes 1048592 | tf_op jit(solution)/shard_map/reduce_scatter | solution.py:314
  1037.0 80.0 %all-reduce.7.cloned.1.call-done = (f32[8,16,2048]{2,1,0:T(8,128)}, f32[8,16,2048]{2,1,0:T(8,128)}, f32[8,16,2048]{2,1,0:T(8,128)}, f32[8,16,2048]{2,1,0:T(8,128)}) async-done(((f32[8,16,2048]{2,1,0:T(8,128)}, f32[8,16,2048]{2,1,0:T(8,128)}, f32[8,16,2048]{2,1,0:T(8,128)}, f32[8,16,2048]{2,1,0:T(8,128)}), (f32[8,16,2048]{2,1,0:T(8,128)}, f32[8,16,2048]{2,1,0:T(8,128)}, f32[8,16,2048]{2,1,0:T(8,128)}, ...) | async-done | bytes 4194320 | tf_op jit(solution)/shard_map/psum | solution.py:323
  (290 shorter events, 146.8 us)
Async XLA Ops:
  7.2 142.1 %copy-start = (bf16[512,2048]{1,0:T(8,128)(2,1)S(1)}, bf16[512,2048]{1,0:T(8,128)(2,1)}, u32[]{:S(2)}) copy-start(bf16[512,2048]{1,0:T(8,128)(2,1)} %param.28) | copy-start | bytes 6291460
  7.2 91.3 %all-gather.5.cloned.1.call-start = ((), (), s32[]{:S(2)}) async-start(), calls=%async_computation.4 | async-start | bytes 5242880 | tf_op jit(solution)/shard_map/all_gather | solution.py:216
  8.9 17.9 %copy-start.64 = (f32[256]{0:T(256)}, f32[256]{0:T(256)S(1)}, u32[]{:S(2)}) copy-start(f32[256]{0:T(256)S(1)} %broadcast_multiply_fusion.9) | copy-start | bytes 3076
  10.5 16.2 %copy-start.66 = (f32[256]{0:T(256)}, f32[256]{0:T(256)S(1)}, u32[]{:S(2)}) copy-start(f32[256]{0:T(256)S(1)} %add_rsqrt_fusion.1) | copy-start | bytes 3076
  11.4 15.4 %copy-start.52 = (f32[1,2048]{1,0:T(1,128)}, f32[1,2048]{1,0:T(1,128)S(1)}, u32[]{:S(2)}) copy-start(f32[1,2048]{1,0:T(1,128)S(1)} %get-tuple-element.32) | copy-start | bytes 24580
  14.9 217.9 %reduce-scatter.5.cloned.1.call-start = ((), (), s32[]{:S(2)}) async-start(), calls=%async_computation.5 | async-start | bytes 5242880 | tf_op jit(solution)/shard_map/reduce_scatter | solution.py:234
  17.7 14.4 %copy-start.38 = (bf16[8,16,2048]{2,1,0:T(8,128)(2,1)S(1)}, bf16[8,16,2048]{2,1,0:T(8,128)(2,1)}, u32[]{:S(2)}) copy-start(bf16[8,16,2048]{2,1,0:T(8,128)(2,1)} %param.37) | copy-start | bytes 1572868
  31.7 206.4 %copy-start.55 = (bf16[1,4,8]{2,1,0:T(4,128)(2,1)}, bf16[1,4,8]{2,1,0:T(4,128)(2,1)S(1)}, u32[]{:S(2)}) copy-start(bf16[1,4,8]{2,1,0:T(4,128)(2,1)S(1)} %get-tuple-element.51) | copy-start | bytes 196
  31.9 117.1 %copy-start.56 = (bf16[1,16,512]{2,0,1:T(2,128)(2,1)}, bf16[1,16,512]{2,0,1:T(2,128)(2,1)S(1)}, u32[]{:S(2)}) copy-start(bf16[1,16,512]{2,0,1:T(2,128)(2,1)S(1)} %fusion.65) | copy-start | bytes 49156
  32.2 78.7 %copy-start.40 = (bf16[1,16,1536]{2,0,1:T(2,128)(2,1)}, bf16[1,16,1536]{2,0,1:T(2,128)(2,1)S(1)}, u32[]{:S(2)}) copy-start(bf16[1,16,1536]{2,0,1:T(2,128)(2,1)S(1)} %fusion.89) | copy-start | bytes 147460
  34.1 67.9 %copy-start.34 = (bf16[1,16,2048]{2,0,1:T(2,128)(2,1)}, bf16[1,16,2048]{2,0,1:T(2,128)(2,1)S(1)}, u32[]{:S(2)}) copy-start(bf16[1,16,2048]{2,0,1:T(2,128)(2,1)S(1)} %fusion.59) | copy-start | bytes 196612
  125.8 14.7 %copy-start.16 = (bf16[1,1024,1,4,128]{4,3,2,1,0:T(4,128)(2,1)}, bf16[1,1024,1,4,128]{4,3,2,1,0:T(4,128)(2,1)S(1)}, u32[]{:S(2)}) copy-start(bf16[1,1024,1,4,128]{4,3,2,1,0:T(4,128)(2,1)S(1)} %get-tuple-element.29) | copy-start | bytes 3145732
  157.3 75.5 %copy-start.3 = (bf16[256,2048]{1,0:T(8,128)(2,1)S(1)}, bf16[256,2048]{1,0:T(8,128)(2,1)}, u32[]{:S(2)}) copy-start(bf16[256,2048]{1,0:T(8,128)(2,1)} %param.22) | copy-start | bytes 3145732
  157.3 75.5 %copy-start.51 = (f32[2048]{0:T(1024)S(1)}, f32[2048]{0:T(1024)}, u32[]{:S(2)}) copy-start(f32[2048]{0:T(1024)} %param.29) | copy-start | bytes 24580
  157.4 158.4 %all-gather.9.cloned.1.call-start = ((), (), s32[]{:S(2)}) async-start(), calls=%async_computation.8 | async-start | bytes 5242880 | tf_op jit(solution)/shard_map/all_gather | solution.py:269
  158.1 239.1 %all-gather.7.cloned.1.call-start = ((), (), s32[]{:S(2)}) async-start(), calls=%async_computation.6 | async-start | bytes 5242880 | tf_op jit(solution)/shard_map/all_gather | solution.py:246
  238.0 288.2 %reduce-scatter.9.cloned.1.call-start = ((), (), s32[]{:S(2)}) async-start(), calls=%async_computation.9 | async-start | bytes 5242880 | tf_op jit(solution)/shard_map/reduce_scatter | solution.py:282
  245.6 151.6 %copy-start.36 = (bf16[1,16,2048]{2,0,1:T(2,128)(2,1)}, bf16[1,16,2048]{2,0,1:T(2,128)(2,1)S(1)}, u32[]{:S(2)}) copy-start(bf16[1,16,2048]{2,0,1:T(2,128)(2,1)S(1)} %fusion.55) | copy-start | bytes 196612
  414.1 22.5 %slice-start.4 = ((s8[8388608]{0:T(1024)(128)(4,1)}), s8[4194304]{0:T(1024)(128)(4,1)S(1)}, s32[]{:S(2)}) async-start(s8[8388608]{0:T(1024)(128)(4,1)} %bitcast.266), calls=%async_computation.19 | async-start | bytes 8388608
  450.8 154.9 %reduce-scatter.7.cloned.1.call-start = ((), (), s32[]{:S(2)}) async-start(), calls=%async_computation.7 | async-start | bytes 5242880 | tf_op jit(solution)/shard_map/reduce_scatter | solution.py:260
  472.2 54.1 %copy-start.63 = (f32[256]{0:T(256)S(1)}, f32[256]{0:T(256)}, u32[]{:S(2)}) copy-start(f32[256]{0:T(256)} %copy-done.62) | copy-start | bytes 3076
  472.2 54.1 %copy-start.69 = (f32[256]{0:T(256)S(1)}, f32[256]{0:T(256)}, u32[]{:S(2)}) copy-start(f32[256]{0:T(256)} %copy-done.68) | copy-start | bytes 3076
  472.2 133.5 %copy-start.70 = (f32[2048]{0:T(1024)S(1)}, f32[2048]{0:T(1024)}, u32[]{:S(2)}) copy-start(f32[2048]{0:T(1024)} %param.33) | copy-start | bytes 24580
  472.2 220.7 %all-gather.11.cloned.1.call-start = ((), (), s32[]{:S(2)}) async-start(), calls=%async_computation.10 | async-start | bytes 5242880 | tf_op jit(solution)/shard_map/all_gather | solution.py:291
  528.6 85.8 %copy-start.50 = (f32[16,1024]{1,0:T(8,128)S(1)}, f32[16,1024]{1,0:T(8,128)}, u32[]{:S(2)}) copy-start(f32[16,1024]{1,0:T(8,128)} %fusion.74) | copy-start | bytes 196612
  611.4 279.1 %all-reduce.9.cloned.1.call-start = ((), (), s32[]{:S(2)}) async-start(), calls=%async_computation.13 | async-start | bytes 8388608 | tf_op jit(solution)/shard_map/psum | solution.py:324
  735.8 217.2 %all-reduce.11.cloned.1.call-start = ((), (), s32[]{:S(2)}) async-start(), calls=%async_computation.14 | async-start | bytes 3145728 | tf_op jit(solution)/shard_map/psum | solution.py:336
  744.7 286.7 %reduce-scatter.11.cloned.1.call-start = ((), (), s32[]{:S(2)}) async-start(), calls=%async_computation.11 | async-start | bytes 5242880 | tf_op jit(solution)/shard_map/reduce_scatter | solution.py:314
  760.8 356.2 %all-reduce.7.cloned.1.call-start = ((), (), s32[]{:S(2)}) async-start(), calls=%async_computation.12 | async-start | bytes 8388608 | tf_op jit(solution)/shard_map/psum | solution.py:323
  890.5 140.9 %copy-start.53 = (f32[1,2048]{1,0:T(1,128)S(1)}, f32[1,2048]{1,0:T(1,128)}, u32[]{:S(2)}) copy-start(f32[1,2048]{1,0:T(1,128)} %copy-done.52) | copy-start | bytes 24580
  890.5 140.9 %copy-start.65 = (f32[256]{0:T(256)S(1)}, f32[256]{0:T(256)}, u32[]{:S(2)}) copy-start(f32[256]{0:T(256)} %copy-done.64) | copy-start | bytes 3076
  890.5 140.9 %copy-start.67 = (f32[256]{0:T(256)S(1)}, f32[256]{0:T(256)}, u32[]{:S(2)}) copy-start(f32[256]{0:T(256)} %copy-done.66) | copy-start | bytes 3076
  (64 other events, 362.9 us)
Sparse Core Ops, SparseCore 0:
  15.0 83.4 all-gather.4
  157.5 75.2 reduce-scatter.4
  234.5 81.2 all-gather.8
  317.8 79.2 all-gather.6
  450.9 75.2 reduce-scatter.8
  528.4 77.2 reduce-scatter.6
  611.5 81.2 all-gather.10
  735.9 154.5 all-reduce.8
  894.6 58.2 all-reduce.10
  955.2 76.1 reduce-scatter.10
  1034.9 82.0 all-reduce.6
